TPU v7x, 128 devices: a whole 4x4x4 slice. The times are simulated.
128 devices in a mesh: dp: 8 (over x, core), fsdp: 16 (over z, y).
Axes of the slice: x: 4, y: 4, z: 4, core: 2. Of those that a mesh axis runs over, the one named last changes fastest.
Arguments:
- tokens: bfloat16 [65536, 1408], P(('dp', 'fsdp')), may hold values from -6 to 6
- image_of: int32 [65536], P(('dp', 'fsdp')), may hold values from 0 to 16383, as said below
- live: int32 [65536], P(('dp', 'fsdp')), may hold values from 0 to 1, as said below
- request_of: int32 [16384], P('dp'), may hold values from -1 to 63, as said below
- ln1_gain: float32 [1408], replicated, may hold values from 0.5 to 1.5
- ln1_shift: float32 [1408], replicated, may hold values from -3 to 3
- w_qkv: bfloat16 [1408, 4224], P('fsdp')
- b_qkv: float32 [4224], replicated, may hold values from -3 to 3
- w_out: bfloat16 [1408, 1408], P('fsdp'), may hold values from -0.15625 to 0.15625
- b_out: float32 [1408], replicated, may hold values from -3 to 3
- ln2_gain: float32 [1408], replicated, may hold values from 0.5 to 1.5
- ln2_shift: float32 [1408], replicated, may hold values from -3 to 3
- w_proj: bfloat16 [5632, 4096], P(None, 'fsdp'), may hold values from -0.078125 to 0.078125
- b_proj: float32 [4096], P('fsdp'), may hold values from -3 to 3
Outputs:
- features: bfloat16 [16384, 4096], P('dp', 'fsdp')
- peaks: float32 [64], replicated
Inputs may be any that keep to these rules, and one draw needn't show every extreme that they name: `image_of`: tokens come in aligned groups of 4 of one image; an image's tokens are consecutive and lie within one aligned block of 512 rows; numbers never fall along the rows; the last block's last group of 4 is an image of its own. Padding fills whole groups of 4 at the end of each aligned block of 512 rows, at most half of the block; the first group of every block is live and the last block has none; a padding token carries the image number of the token before it. `request_of`: -1 exactly on merged rows of padding; on the other rows request numbers never fall along the rows, and every request has some row.
All inputs are finite; a program needn't handle non-finite values.
Results may differ from a plain program's by a relative error of at most 0.012.
The roundings to bfloat16 on the way count: a program that leaves them out, or rounds other values in their place, can miss the bound.
Values may be sent and summed in bfloat16 or wider, within the bound.
A program may use at most 192 MiB of HBM per device.

v0:
```python
import jax
import jax.numpy as jnp
from jax import lax
from jax.sharding import PartitionSpec as P

HEADS = 16


def normalize(values, gain, shift):
    mean_value = jnp.mean(values, axis=-1, keepdims=True)
    centred = values - mean_value
    variance = jnp.mean(centred * centred, axis=-1, keepdims=True)
    return centred * lax.rsqrt(variance + 1e-06) * gain + shift


def attention(qkv, image_ids, live_flags, heads):
    count_rows = qkv.shape[0]
    width = qkv.shape[1] // 3
    head_size = width // heads
    scale = head_size ** (-0.5)
    queries = qkv[:, :width].reshape(count_rows, heads, head_size)
    keys_all = qkv[:, width : 2 * width].reshape(count_rows, heads, head_size)
    values_all = qkv[:, 2 * width :].reshape(count_rows, heads, head_size)
    block_rows = min(512, count_rows)
    blocks = count_rows // block_rows
    key_live = live_flags[None, :] == 1

    def one_block(items):
        block_queries, block_images = items
        scores = (
            jnp.einsum("qhe,khe->hqk", block_queries, keys_all, preferred_element_type=jnp.float32)
            * scale
        )
        allowed = (block_images[:, None] == image_ids[None, :]) & key_live
        scores = jnp.where(allowed[None], scores, jnp.float32(-1e30))
        top = jnp.max(scores, axis=-1, keepdims=True)
        expo = jnp.exp(scores - top)
        weights = (expo / jnp.sum(expo, axis=-1, keepdims=True)).astype(jnp.bfloat16)
        mixed = jnp.einsum("hqk,khe->qhe", weights, values_all, preferred_element_type=jnp.float32)
        return mixed.reshape(block_rows, width).astype(jnp.bfloat16)

    result = lax.map(
        one_block,
        (
            queries.reshape(blocks, block_rows, heads, head_size),
            image_ids.reshape(blocks, block_rows),
        ),
    )
    return result.reshape(count_rows, width)


def shards(
    tokens,
    image_of,
    live,
    request_of,
    ln1_gain,
    ln1_shift,
    w_qkv,
    b_qkv,
    w_out,
    b_out,
    ln2_gain,
    ln2_shift,
    w_proj,
    b_proj,
):
    count_rows = tokens.shape[0]
    width = tokens.shape[1]
    resid = tokens.astype(jnp.float32)
    normed = normalize(resid, ln1_gain, ln1_shift).astype(jnp.bfloat16)
    columns = normed
    mixed = jnp.dot(
        columns,
        lax.all_gather(w_qkv, "fsdp", axis=0, tiled=True),
        preferred_element_type=jnp.float32,
    )
    qkv = (mixed + b_qkv).astype(jnp.bfloat16)
    attended = attention(qkv, image_of, live, HEADS)
    columns = attended
    projected_out = jnp.dot(
        columns,
        lax.all_gather(w_out, "fsdp", axis=0, tiled=True),
        preferred_element_type=jnp.float32,
    )
    resid = resid + (projected_out + b_out)
    normed2 = normalize(resid, ln2_gain, ln2_shift).astype(jnp.bfloat16)
    merged = normed2.reshape(count_rows // 4, 4 * width)
    projected = (
        jnp.dot(
            lax.all_gather(merged, "fsdp", axis=0, tiled=True),
            w_proj,
            preferred_element_type=jnp.float32,
        )
        + b_proj
    )
    requests = lax.axis_size("dp") * lax.axis_size("fsdp") // 2
    columns_here = projected.shape[1]
    labels = jnp.arange(requests, dtype=jnp.int32)
    member = request_of[:, None] == labels[None, :]
    row_squares = jnp.sum(projected * projected, axis=1)
    row_top = jnp.max(projected, axis=1)
    sums_part = jnp.sum(jnp.where(member, row_squares[:, None], jnp.float32(0.0)), axis=0)
    entries_part = jnp.sum(member.astype(jnp.float32), axis=0) * jnp.float32(columns_here)
    top_part = jnp.max(jnp.where(member, row_top[:, None], jnp.float32(-jnp.inf)), axis=0)
    sumsq, entries = lax.psum((sums_part, entries_part), ("dp", "fsdp"))
    top = lax.pmax(top_part, ("dp", "fsdp"))
    rms = jnp.sqrt(sumsq / entries + 1e-06)
    valid = request_of >= 0
    row_rms = jnp.sum(jnp.where(member, rms[None, :], jnp.float32(0.0)), axis=1) + jnp.where(
        valid, 0.0, 1.0
    )
    features = jnp.where(valid[:, None], projected / row_rms[:, None], jnp.float32(0.0)).astype(
        jnp.bfloat16
    )
    peaks = top / rms
    return (features, peaks)


def solution(mesh):
    return jax.shard_map(
        shards,
        mesh=mesh,
        in_specs=(
            P(("dp", "fsdp"), None),
            P(("dp", "fsdp")),
            P(("dp", "fsdp")),
            P("dp"),
            P(),
            P(),
            P("fsdp", None),
            P(),
            P("fsdp", None),
            P(),
            P(),
            P(),
            P(None, "fsdp"),
            P("fsdp"),
        ),
        out_specs=(P("dp", "fsdp"), P()),
        check_vma=False,
    )
```

profile of v0, /device:TPU:1, one launch (start us, length us, event | category | flops | bytes accessed | tf_op | source)
XLA Modules:
  0.0 461.9 jit_solution(2938531197813447947)
XLA Ops:
  7.3 0.7 all-gather.4.cloned.1.call-update
  8.0 0.7 all-gather.6.cloned.1.call-update
  8.8 1.6 convert_reduce_fusion
  10.4 1.9 fusion.8
  12.6 87.9 %all-gather.4.cloned.1.call-done = bf16[1408,4224]{1,0:T(8,128)(2,1)} async-done(((bf16[88,4224]{1,0:T(8,128)(2,1)}), bf16[1408,4224]{1,0:T(8,128)(2,1)}) %all-gather.4.cloned.1.call-update) | async-done | bytes 11894800 | tf_op jit(solution)/shard_map/all_gather | solution.py:75
  100.5 12.4 %add_convert_fusion = bf16[512,4224]{1,0:T(8,128)(2,1)S(1)} fusion(bf16[1408,4224]{1,0:T(8,128)(2,1)} %all-gather.4.cloned.1.call-done, f32[4224]{0:T(1024)S(1)} %copy-done.7, bf16[512,1408]{1,0:T(8,128)(2,1)} %param.14, f32[1408]{0:T(1024)S(1)} %copy-done.8, f32[1408]{0:T(1024)S(1)} %copy-done.9, f32[512]{0:T(512)S(1)} %add_rsqrt_fusion.1, ...), kind=kOutput, calls=%fused_computation.5 | convolution fusion | flops 6098780160 | bytes 17694208 | tf_op jit(solution)/shard_map/dot_general | solution.py:73
  112.8 2.1 fusion.23
  115.0 2.6 copy.27
  117.6 2.5 copy.28
  120.1 2.6 copy.26
  122.7 11.0 %fusion.24 = (f32[16,512]{1,0:T(8,128)S(1)}, f32[16,512,512]{1,2,0:T(8,128)}) fusion(pred[512,512]{0,1:T(8,128)(4,1)S(1)} %compare_and_fusion, bf16[512,16,88]{0,2,1:T(8,128)(2,1)} %bitcast.17, bf16[512,16,88]{0,2,1:T(8,128)(2,1)} %bitcast.18), kind=kOutput, calls=%fused_computation.50 | convolution fusion | flops 754975232 | bytes 19955712 | tf_op jit(solution)/shard_map/while/body/eval_jaxpr/sub | solution.py:37
  133.7 8.9 %fusion.14 = bf16[16,88,512]{2,1,0:T(8,128)(2,1)} fusion(bf16[512,16,88]{0,2,1:T(8,128)(2,1)} %bitcast.19, f32[16,512,512]{1,2,0:T(8,128)} %get-tuple-element.46, f32[16,512]{1,0:T(8,128)S(1)} %get-tuple-element.45), kind=kOutput, calls=%fused_computation.26 | convolution fusion | flops 747307008 | bytes 19693568 | tf_op jit(solution)/shard_map/while/body/eval_jaxpr/hqk,khe->qhe/dot_general | solution.py:39
  142.5 10.3 %all-gather.6.cloned.1.call-done = bf16[1408,1408]{1,0:T(8,128)(2,1)} async-done(((bf16[88,1408]{1,0:T(8,128)(2,1)}), bf16[1408,1408]{1,0:T(8,128)(2,1)}) %all-gather.6.cloned.1.call-update) | async-done | bytes 3964944 | tf_op jit(solution)/shard_map/all_gather | solution.py:83
  152.9 5.9 %fusion.25 = (f32[512]{0:T(512)S(1)}, f32[512,1408]{1,0:T(8,128)S(1)}) fusion(f32[1408]{0:T(1024)S(1)} %copy-done.2, bf16[512,1408]{0,1:T(8,128)(2,1)} %bitcast.16, bf16[1408,1408]{1,0:T(8,128)(2,1)} %all-gather.6.cloned.1.call-done, bf16[512,1408]{1,0:T(8,128)(2,1)} %param.14), kind=kOutput, calls=%fused_computation.51 | convolution fusion | flops 2032926208 | bytes 9739776 | tf_op jit(solution)/shard_map/dot_general | solution.py:81
  158.8 0.4 multiply_reduce_fusion
  159.5 1.7 add_convert_fusion.1
  161.2 3.6 reshape.109
  164.8 143.3 %all-gather.8.cloned.1.call-done = bf16[2048,5632]{1,0:T(8,128)(2,1)} async-done(((bf16[128,5632]{1,0:T(8,128)(2,1)}), bf16[2048,5632]{1,0:T(8,128)(2,1)}) %all-gather.8.cloned.1.call-update) | async-done | bytes 23068688 | tf_op jit(solution)/shard_map/all_gather | solution.py:91
  308.2 12.5 %fusion.22 = (f32[2048]{0:T(1024)S(1)}, f32[2048]{0:T(1024)S(1)}, f32[2048,256]{0,1:T(8,128)}) fusion(f32[256]{0:T(256)S(1)} %copy-done.10, bf16[2048,5632]{1,0:T(8,128)(2,1)} %all-gather.8.cloned.1.call-done, bf16[5632,256]{1,0:T(8,128)(2,1)S(1)} %copy-done), kind=kOutput, calls=%fused_computation.48 | convolution fusion | flops 5907673088 | bytes 28066816 | tf_op jit(solution)/shard_map/dot_general | solution.py:90
  320.9 64.6 %all-reduce = (f32[64]{0:T(128)S(1)}, f32[64]{0:T(128)S(1)}) all-reduce(f32[64]{0:T(128)S(1)} %get-tuple-element.37, f32[64]{0:T(128)S(1)} %broadcast_multiply_fusion.2), channel_id=1, replica_groups=mesh['dp'=8,'fsdp'=16] {'dp','fsdp'}, use_global_device_ids=true, to_apply=%region_8.9 | all-reduce | flops 128 | bytes 1024 | tf_op jit(solution)/shard_map/psum | solution.py:106
  385.7 64.1 %pmax.7 = f32[64]{0:T(128)S(1)} all-reduce(f32[64]{0:T(128)S(1)} %get-tuple-element.34), channel_id=1, replica_groups=mesh['dp'=8,'fsdp'=16] {'dp','fsdp'}, use_global_device_ids=true, to_apply=%region_14.15 | all-reduce | flops 64 | bytes 512 | tf_op jit(solution)/shard_map/pmax | solution.py:107
  449.8 0.5 div.47
  450.3 2.8 select_convert_fusion
  453.2 2.3 copy.30
  (37 shorter events, 1.1 us)
Async XLA Ops:
  7.2 301.0 %copy-start = (bf16[5632,256]{1,0:T(8,128)(2,1)S(1)}, bf16[5632,256]{1,0:T(8,128)(2,1)}, u32[]{:S(2)}) copy-start(bf16[5632,256]{1,0:T(8,128)(2,1)} %param.26) | copy-start | bytes 8650756
  7.2 5.1 %copy-start.6 = (s32[512]{0:T(512)S(1)}, s32[512]{0:T(512)}, u32[]{:S(2)}) copy-start(s32[512]{0:T(512)} %param.16) | copy-start | bytes 6148
  7.2 5.1 %copy-start.5 = (s32[512]{0:T(512)S(1)}, s32[512]{0:T(512)}, u32[]{:S(2)}) copy-start(s32[512]{0:T(512)} %param.15) | copy-start | bytes 6148
  7.2 93.3 %copy-start.9 = (f32[1408]{0:T(1024)S(1)}, f32[1408]{0:T(1024)}, u32[]{:S(2)}) copy-start(f32[1408]{0:T(1024)} %param.18) | copy-start | bytes 16900
  7.2 93.3 %copy-start.8 = (f32[1408]{0:T(1024)S(1)}, f32[1408]{0:T(1024)}, u32[]{:S(2)}) copy-start(f32[1408]{0:T(1024)} %param.19) | copy-start | bytes 16900
  7.2 93.3 %copy-start.7 = (f32[4224]{0:T(1024)S(1)}, f32[4224]{0:T(1024)}, u32[]{:S(2)}) copy-start(f32[4224]{0:T(1024)} %param.21) | copy-start | bytes 50692
  7.2 93.2 %all-gather.4.cloned.1.call-start = ((), (), s32[]{:S(2)}) async-start(), calls=%async_computation | async-start | bytes 12638208 | tf_op jit(solution)/shard_map/all_gather | solution.py:75
  8.0 144.9 %all-gather.6.cloned.1.call-start = ((), (), s32[]{:S(2)}) async-start(), calls=%async_computation.1 | async-start | bytes 4212736 | tf_op jit(solution)/shard_map/all_gather | solution.py:83
  8.7 299.4 %all-gather.8.cloned.1.call-start = ((), (), s32[]{:S(2)}) async-start(), calls=%async_computation.2 | async-start | bytes 24510464 | tf_op jit(solution)/shard_map/all_gather | solution.py:91
  133.7 19.2 %copy-start.2 = (f32[1408]{0:T(1024)S(1)}, f32[1408]{0:T(1024)}, u32[]{:S(2)}) copy-start(f32[1408]{0:T(1024)} %param.23) | copy-start | bytes 16900
  158.8 0.7 copy-start.3
  158.8 0.7 copy-start.4
  161.2 147.0 %copy-start.10 = (f32[256]{0:T(256)S(1)}, f32[256]{0:T(256)}, u32[]{:S(2)}) copy-start(f32[256]{0:T(256)} %param.27) | copy-start | bytes 3076
  164.8 155.8 %copy-start.1 = (s32[2048]{0:T(1024)S(1)}, s32[2048]{0:T(1024)}, u32[]{:S(2)}) copy-start(s32[2048]{0:T(1024)} %param.17) | copy-start | bytes 24580
Sparse Core Ops, SparseCore 0:
  10.2 90.2 all-gather.3
  102.6 50.2 all-gather.5
  164.9 143.1 all-gather.7
where the time goes:
time: 462 us
  waiting for transfers between devices  243 us (53%)
  blocking collectives  129 us (28%)
  matrix products  50.6 us (11%)
  local copies, waits for them, and re-layouts  16 us (3%)
  between operations  13.9 us (3%)
  other arithmetic  9.62 us (2%)
    all_gather x1, waiting for transfers between devices, shards(): lax.all_gather(merged, 'fsdp', axis=0, tiled=True)  143 us
    all_gather x1, waiting for transfers between devices, shards(): lax.all_gather(w_qkv, 'fsdp', axis=0, tiled=True)  87.9 us
    psum x1, blocking collectives, shards(): sumsq, entries = lax.psum((sums_part, entries_part), ('dp', 'fsdp'))  64.6 us
    pmax x1, blocking collectives, shards(): top = lax.pmax(top_part, ('dp', 'fsdp'))  64.1 us
    dot_general x1, matrix products, shards(): jnp.dot(lax.all_gather(merged, 'fsdp', axis=0, tiled=True), w_proj, prefe...  12.5 us
    dot_general x1, matrix products, shards(): jnp.dot(columns, lax.all_gather(w_qkv, 'fsdp', axis=0, tiled=True), prefe...  12.4 us
    sub x1, matrix products, one_block(): expo = jnp.exp(scores - top)  11 us
    all_gather x1, waiting for transfers between devices, shards(): lax.all_gather(w_out, 'fsdp', axis=0, tiled=True)  10.3 us
  transfers between devices with their start and end apart: 3, of which 3 were waited for; matrix products, arithmetic and copies ran while one was open for 10% of the time, Pallas kernels for 0%

commit v1 on v0

v1 whole, which is shorter than its diff:
```python
import functools

import jax
import jax.numpy as jnp
from jax import lax
from jax.experimental import pallas as pl
from jax.experimental.pallas import tpu as pltpu
from jax.sharding import PartitionSpec as P

HEADS = 16
REQUESTS = 64
MESH = pl.DeviceIdType.MESH


def normalize(values, gain, shift):
    mean_value = jnp.mean(values, axis=-1, keepdims=True)
    centred = values - mean_value
    variance = jnp.mean(centred * centred, axis=-1, keepdims=True)
    return centred * lax.rsqrt(variance + 1e-06) * gain + shift


def attention(qkv, image_ids, live_flags, heads):
    count_rows = qkv.shape[0]
    width = qkv.shape[1] // 3
    head_size = width // heads
    scale = head_size ** (-0.5)
    queries = qkv[:, :width].reshape(count_rows, heads, head_size)
    keys_all = qkv[:, width : 2 * width].reshape(count_rows, heads, head_size)
    values_all = qkv[:, 2 * width :].reshape(count_rows, heads, head_size)
    key_live = live_flags[None, :] == 1
    scores = jnp.einsum("qhe,khe->hqk", queries, keys_all, preferred_element_type=jnp.float32) * scale
    allowed = (image_ids[:, None] == image_ids[None, :]) & key_live
    scores = jnp.where(allowed[None], scores, jnp.float32(-1e30))
    top = jnp.max(scores, axis=-1, keepdims=True)
    expo = jnp.exp(scores - top)
    weights = (expo / jnp.sum(expo, axis=-1, keepdims=True)).astype(jnp.bfloat16)
    mixed = jnp.einsum("hqk,khe->qhe", weights, values_all, preferred_element_type=jnp.float32)
    return mixed.reshape(count_rows, width).astype(jnp.bfloat16)


class Copies:
    def __init__(self, send_sems, recv_sems, local_sems):
        self.send_sems, self.recv_sems, self.local_sems = send_sems, recv_sems, local_sems
        self.remote_count = 0
        self.local_count = 0
        self.sent = []

    def remote(self, src, dst, to):
        index = self.remote_count
        self.remote_count += 1
        copy = pltpu.make_async_remote_copy(
            src_ref=src,
            dst_ref=dst,
            send_sem=self.send_sems.at[index],
            recv_sem=self.recv_sems.at[index],
            device_id=to,
            device_id_type=MESH,
        )
        copy.start()
        self.sent.append(copy)
        return copy

    def local(self, src, dst):
        index = self.local_count
        self.local_count += 1
        copy = pltpu.make_async_copy(src, dst, self.local_sems.at[index])
        copy.start()
        return copy


def column_of(row):
    n = row.shape[1]
    wide = jnp.broadcast_to(row, (n, n))
    diagonal = lax.broadcasted_iota(jnp.int32, (n, n), 0) == lax.broadcasted_iota(jnp.int32, (n, n), 1)
    return jnp.sum(jnp.where(diagonal, wide, 0), axis=1, keepdims=True)


def project_kernel(
    merged_hbm, weight_hbm, bias_hbm, request_ref, out_hbm, stats_ref,
    mbuf, wbuf, bbuf, stage, squares, tops, first, second,
    send_sems, recv_sems, local_sems,
):
    d, f = lax.axis_index("dp"), lax.axis_index("fsdp")
    z, y = f // 4, f % 4
    core = d % 2
    partner = (d + 1 - 2 * core, f)

    def at_y(step):
        return (d, z * 4 + (y + step + 4) % 4)

    def at_z(step):
        return (d, ((z + step + 4) % 4) * 4 + y)

    barrier = pltpu.get_barrier_semaphore()
    for step in range(1, 16):
        pl.semaphore_signal(barrier, inc=1, device_id=(d, (f + step) % 16), device_id_type=MESH)
    for step in range(1, 8):
        pl.semaphore_signal(barrier, inc=1, device_id=((d + step) % 8, f), device_id_type=MESH)
    copies = Copies(send_sems, recv_sems, local_sems)
    loads = [copies.local(weight_hbm, wbuf.at[0]), copies.local(merged_hbm, mbuf.at[0]), copies.local(bias_hbm, bbuf.at[0])]
    pl.semaphore_wait(barrier, 22)

    own = [2 * core, 2 * core + 1]
    w_right = [copies.remote(weight_hbm.at[own[k]], wbuf.at[3, own[k]], at_y(1)) for k in (0, 1)]
    w_left = [copies.remote(weight_hbm.at[own[k]], wbuf.at[1, own[k]], at_y(-1)) for k in (1, 0)][::-1]
    m_up = [copies.remote(merged_hbm.at[s], mbuf.at[3, s], at_z(1)) for s in (0, 1, 2, 3)]
    m_down = {s: copies.remote(merged_hbm.at[s], mbuf.at[1, s], at_z(-1)) for s in (2, 3, 0, 1)}
    b_all = {r: copies.remote(bias_hbm, bbuf.at[4 - r], at_y(r)) for r in (1, 2, 3)}
    for load in loads:
        load.wait()

    lane = lax.broadcasted_iota(jnp.int32, (128, 128), 1)

    def block(rz, ry):
        total = jnp.dot(mbuf[rz, 0], wbuf[ry, 0], preferred_element_type=jnp.float32)
        for s in range(1, 4):
            total += jnp.dot(mbuf[rz, s], wbuf[ry, s], preferred_element_type=jnp.float32)
        total += bbuf[ry]
        stage[rz, ry] = total.astype(jnp.bfloat16)
        left, right = total[:, :128], total[:, 128:]
        return left * left + right * right, jnp.maximum(left, right)

    outs, stored = [], []

    def first_block(rz, ry):
        squares[rz], tops[rz] = block(rz, ry)

    def more_block(rz, ry):
        square, top = block(rz, ry)
        squares[rz] = squares[rz] + square
        tops[rz] = jnp.maximum(tops[rz], top)

    def hand_over(rz, ry):
        row_block = ((z + rz) % 4) * 4 + y
        if ry == 0:
            stored.append(copies.local(stage.at[rz, ry], out_hbm.at[row_block]))
        else:
            outs.append(copies.remote(stage.at[rz, ry], out_hbm.at[row_block], at_y(ry)))

    first_block(0, 0)
    hand_over(0, 0)

    m_fwd = []
    for k in (0, 1):
        m_up[k].wait_recv()
        m_fwd.append(copies.remote(mbuf.at[3, k], mbuf.at[2, k], at_z(1)))
        m_down[2 + k].wait_recv()
        m_fwd.append(copies.remote(mbuf.at[1, 2 + k], mbuf.at[2, 2 + k], at_z(-1)))
    w_fwd, swap = [], []
    w_right[0].wait_recv()
    w_fwd.append(copies.remote(wbuf.at[3, own[0]], wbuf.at[2, own[0]], at_y(1)))
    swap.append(copies.remote(wbuf.at[3, own[0]], wbuf.at[3, own[0]], partner))
    w_left[1].wait_recv()
    w_fwd.append(copies.remote(wbuf.at[1, own[1]], wbuf.at[2, own[1]], at_y(-1)))
    swap.append(copies.remote(wbuf.at[1, own[1]], wbuf.at[1, own[1]], partner))
    for copy in (m_up[2], m_up[3], m_down[0], m_down[1]):
        copy.wait_recv()
    for rz in (1, 3):
        first_block(rz, 0)
        hand_over(rz, 0)
    w_right[1].wait_recv()
    swap.append(copies.remote(wbuf.at[3, own[1]], wbuf.at[3, own[1]], partner))
    w_left[0].wait_recv()
    swap.append(copies.remote(wbuf.at[1, own[0]], wbuf.at[1, own[0]], partner))
    for copy in swap + list(b_all.values()):
        copy.wait_recv()
    for ry in (1, 3):
        for rz in (0, 1, 3):
            more_block(rz, ry)
            hand_over(rz, ry)
    for copy in m_fwd:
        copy.wait_recv()
    first_block(2, 0)
    hand_over(2, 0)
    for ry in (1, 3):
        more_block(2, ry)
        hand_over(2, ry)
    swap = []
    for k in (0, 1):
        w_fwd[k].wait_recv()
        swap.append(copies.remote(wbuf.at[2, own[k]], wbuf.at[2, own[k]], partner))
    for copy in swap:
        copy.wait_recv()
    for rz in range(4):
        more_block(rz, 2)
        hand_over(rz, 2)

    sums = jnp.zeros((1, 128), jnp.float32)
    entries = jnp.zeros((1, 128), jnp.float32)
    peak = jnp.full((1, 128), -jnp.inf, jnp.float32)
    for rz in range(4):
        row_block = ((z + rz) % 4) * 4 + y
        member = column_of(request_ref[pl.ds(row_block, 1), :]) == lane
        row_square = jnp.sum(squares[rz], axis=1, keepdims=True)
        row_top = jnp.max(tops[rz], axis=1, keepdims=True)
        sums += jnp.sum(jnp.where(member, row_square, 0.0), axis=0, keepdims=True)
        entries += jnp.sum(jnp.where(member, 1024.0, 0.0), axis=0, keepdims=True)
        peak = jnp.maximum(peak, jnp.max(jnp.where(member, row_top, -jnp.inf), axis=0, keepdims=True))

    def pack(sums, entries, peak):
        return jnp.concatenate([sums, entries, peak, jnp.zeros((5, 128), jnp.float32)], axis=0)

    def combine(slots, count):
        total, high = slots[0], slots[0]
        for i in range(1, count):
            total = total + slots[i]
            high = jnp.maximum(high, slots[i])
        return total[0:1], total[1:2], high[2:3]

    first[f] = pack(sums, entries, peak)
    round_one = [copies.remote(first.at[f], first.at[f], (d, (f + step) % 16)) for step in range(1, 16)]
    for copy in round_one:
        copy.wait_recv()
    second[d] = pack(*combine(first, 16))
    round_two = [copies.remote(second.at[d], second.at[d], ((d + step) % 8, f)) for step in range(1, 8)]
    for copy in round_two:
        copy.wait_recv()
    sums, entries, peak = combine(second, 8)
    lanes = lax.broadcasted_iota(jnp.int32, (1, 128), 1)
    rms = jnp.sqrt(sums / jnp.where(lanes < REQUESTS, entries, 1.0) + 1e-06)
    stats_ref[...] = pack(rms, peak / rms, peak)

    for copy in outs:
        copy.wait_recv()
    for copy in stored:
        copy.wait()
    for copy in copies.sent:
        copy.wait_send()


def project(merged, w_proj, b_proj, request_of):
    depth = merged.shape[2]
    any_space = pl.BlockSpec(memory_space=pl.ANY)
    vmem = pl.BlockSpec(memory_space=pltpu.VMEM)
    return pl.pallas_call(
        project_kernel,
        out_shape=(
            jax.ShapeDtypeStruct((16, 128, 256), jnp.bfloat16),
            jax.ShapeDtypeStruct((8, 128), jnp.float32),
        ),
        in_specs=[any_space, any_space, any_space, vmem],
        out_specs=(any_space, vmem),
        scratch_shapes=[
            pltpu.VMEM((4, 4, 128, depth), jnp.bfloat16),
            pltpu.VMEM((4, 4, depth, 256), jnp.bfloat16),
            pltpu.VMEM((4, 1, 256), jnp.float32),
            pltpu.VMEM((4, 4, 128, 256), jnp.bfloat16),
            pltpu.VMEM((4, 128, 128), jnp.float32),
            pltpu.VMEM((4, 128, 128), jnp.float32),
            pltpu.VMEM((16, 8, 128), jnp.float32),
            pltpu.VMEM((8, 8, 128), jnp.float32),
            pltpu.SemaphoreType.DMA((61,)),
            pltpu.SemaphoreType.DMA((61,)),
            pltpu.SemaphoreType.DMA((7,)),
        ],
        compiler_params=pltpu.CompilerParams(
            collective_id=0, has_side_effects=True, vmem_limit_bytes=60 * 1024 * 1024
        ),
        name="project",
    )(merged, w_proj.reshape(4, depth, 256), b_proj.reshape(1, 256), request_of.reshape(16, 128))


def shards(
    tokens, image_of, live, request_of, ln1_gain, ln1_shift, w_qkv, b_qkv,
    w_out, b_out, ln2_gain, ln2_shift, w_proj, b_proj,
):
    count_rows, width = tokens.shape
    resid = tokens.astype(jnp.float32)
    normed = normalize(resid, ln1_gain, ln1_shift).astype(jnp.bfloat16)
    mixed = jnp.dot(normed, lax.all_gather(w_qkv, "fsdp", axis=0, tiled=True), preferred_element_type=jnp.float32)
    qkv = (mixed + b_qkv).astype(jnp.bfloat16)
    attended = attention(qkv, image_of, live, HEADS)
    projected_out = jnp.dot(
        attended, lax.all_gather(w_out, "fsdp", axis=0, tiled=True), preferred_element_type=jnp.float32
    )
    resid = resid + (projected_out + b_out)
    normed2 = normalize(resid, ln2_gain, ln2_shift).astype(jnp.bfloat16)
    merged = normed2.reshape(count_rows // 4, 4, width).transpose(1, 0, 2)
    raw, stats = project(merged, w_proj, b_proj, request_of)
    rms, peaks = stats[0, :REQUESTS], stats[1, :REQUESTS]
    labels = jnp.arange(REQUESTS, dtype=jnp.int32)
    member = request_of[:, None] == labels[None, :]
    valid = request_of >= 0
    row_rms = jnp.sum(jnp.where(member, rms[None, :], 0.0), axis=1) + jnp.where(valid, 0.0, 1.0)
    projected = raw.reshape(raw.shape[0] * raw.shape[1], raw.shape[2]).astype(jnp.float32)
    features = jnp.where(valid[:, None], projected / row_rms[:, None], 0.0).astype(jnp.bfloat16)
    return (features, peaks)


def solution(mesh):
    return jax.shard_map(
        shards,
        mesh=mesh,
        in_specs=(
            P(("dp", "fsdp"), None),
            P(("dp", "fsdp")),
            P(("dp", "fsdp")),
            P("dp"),
            P(),
            P(),
            P("fsdp", None),
            P(),
            P("fsdp", None),
            P(),
            P(),
            P(),
            P(None, "fsdp"),
            P("fsdp"),
        ),
        out_specs=(P("dp", "fsdp"), P()),
        check_vma=False,
    )
```

time: 462 us -> 247 us (0.53)
  waiting for transfers between devices: 243 us -> 105 us
  blocking collectives: 129 us -> 0 us
  Pallas kernels: 0 us -> 74.9 us
  matrix products: 50.6 us -> 35 us
    all_gather x1 -> x0, waiting for transfers between devices: 143 us -> none  [shards(): lax.all_gather(merged, 'fsdp', axis=0, tiled=True)]
    pallas_call x0 -> x1, Pallas kernels: none -> 74.9 us  [project(): pl.pallas_call(project_kernel, out_shape=(jax.ShapeDtypeStruct((16, 128,...]
    psum x1 -> x0, blocking collectives: 64.6 us -> none  [shards(): sumsq, entries = lax.psum((sums_part, entries_part), ('dp', 'fsdp'))]
    pmax x1 -> x0, blocking collectives: 64.1 us -> none  [shards(): top = lax.pmax(top_part, ('dp', 'fsdp'))]
    dot_general x4 -> x3, matrix products: 39.7 us -> 24 us  [the longest x1 10.9 us: shards(): jnp.dot(normed, lax.all_gather(w_qkv, 'fsdp', axis=0, tiled=True), prefer...]
  transfers between devices with their start and end apart: 3 -> 2, of which waited for: 3 -> 2; matrix products, arithmetic and copies ran while one was open for 10% -> 17% of each run, Pallas kernels for 0% -> 0%
where the time goes in v1:
time: 247 us
  waiting for transfers between devices  105 us (43%)
  Pallas kernels  74.9 us (30%)
  matrix products  35 us (14%)
  between operations  14.2 us (6%)
  local copies, waits for them, and re-layouts  11.8 us (5%)
  other arithmetic  6.08 us (2%)
    all_gather x1, waiting for transfers between devices, shards(): lax.all_gather(w_qkv, 'fsdp', axis=0, tiled=True)  89.3 us
    pallas_call x1, Pallas kernels, project(): pl.pallas_call(project_kernel, out_shape=(jax.ShapeDtypeStruct((16, 128,...  74.9 us
    all_gather x1, waiting for transfers between devices, shards(): lax.all_gather(w_out, 'fsdp', axis=0, tiled=True)  13.8 us
    sub x1, matrix products, attention(): expo = jnp.exp(scores - top)  11 us
    dot_general x1, matrix products, shards(): jnp.dot(normed, lax.all_gather(w_qkv, 'fsdp', axis=0, tiled=True), prefer...  10.9 us
    dot_general x1, matrix products, attention(): jnp.einsum('hqk,khe->qhe', weights, values_all, preferred_element_type=jn...  8.03 us
    dot_general x1, matrix products, shards(): jnp.dot(attended, lax.all_gather(w_out, 'fsdp', axis=0, tiled=True), pref...  5.08 us
  transfers between devices with their start and end apart: 2, of which 2 were waited for; matrix products, arithmetic and copies ran while one was open for 17% of the time, Pallas kernels for 0%

profile of v1, /device:TPU:1, one launch (start us, length us, event | category | flops | bytes accessed | tf_op | source)
XLA Modules:
  0.0 246.6 jit_solution(4951938904151884543)
XLA Ops:
  7.3 0.7 all-gather.3.cloned.1.call-update
  8.0 0.7 all-gather.5.cloned.1.call-update
  8.7 1.6 convert_reduce_fusion
  10.4 0.5 fusion.8
  10.9 0.2 compare_and_fusion
  11.2 89.3 %all-gather.3.cloned.1.call-done = bf16[1408,4224]{1,0:T(8,128)(2,1)} async-done(((bf16[88,4224]{1,0:T(8,128)(2,1)}), bf16[1408,4224]{1,0:T(8,128)(2,1)}) %all-gather.3.cloned.1.call-update) | async-done | bytes 11894800 | tf_op jit(solution)/shard_map/all_gather | solution.py:270
  100.5 10.9 %add_convert_fusion = bf16[512,4224]{1,0:T(8,128)(2,1)S(1)} fusion(bf16[1408,4224]{1,0:T(8,128)(2,1)} %all-gather.3.cloned.1.call-done, f32[4224]{0:T(1024)S(1)} %copy-done.7, bf16[512,1408]{1,0:T(8,128)(2,1)S(1)} %copy-done, f32[1408]{0:T(1024)S(1)} %copy-done.8, f32[1408]{0:T(1024)S(1)} %copy-done.9, f32[512]{0:T(512)S(1)} %add_rsqrt_fusion.1, ...), kind=kOutput, calls=%fused_computation.5 | convolution fusion | flops 6098780160 | bytes 17694208 | tf_op jit(solution)/shard_map/dot_general | solution.py:270
  111.4 1.9 fusion.24
  113.3 2.6 %copy.25 = bf16[512,1408]{0,1:T(8,128)(2,1)} copy(bf16[512,1408]{1,0:T(8,128)(2,1)} %get-tuple-element.10) | data formatting | bytes 2883584 | tf_op jit(solution)/shard_map/slice | solution.py:29
  115.9 2.6 %copy.26 = bf16[512,1408]{0,1:T(8,128)(2,1)} copy(bf16[512,1408]{1,0:T(8,128)(2,1)} %get-tuple-element.9) | data formatting | bytes 2883584 | tf_op jit(solution)/shard_map/slice | solution.py:27
  118.5 1.6 copy.27
  120.0 11.0 %fusion.25 = (f32[16,512]{1,0:T(8,128)S(1)}, f32[16,512,512]{1,2,0:T(8,128)}) fusion(pred[512,512]{0,1:T(8,128)(4,1)S(1)} %compare_and_fusion, bf16[512,16,88]{0,2,1:T(8,128)(2,1)} %bitcast.31, bf16[512,16,88]{0,2,1:T(8,128)(2,1)} %bitcast.32), kind=kOutput, calls=%fused_computation.47 | convolution fusion | flops 754975232 | bytes 19955712 | tf_op jit(solution)/shard_map/sub | solution.py:35
  131.0 8.0 %fusion.16 = bf16[16,88,512]{2,1,0:T(8,128)(2,1)S(1)} fusion(bf16[512,16,88]{0,2,1:T(8,128)(2,1)} %bitcast.30, f32[16,512,512]{1,2,0:T(8,128)} %get-tuple-element.14, f32[16,512]{1,0:T(8,128)S(1)} %get-tuple-element.13), kind=kOutput, calls=%fused_computation.26 | convolution fusion | flops 747307008 | bytes 19693568 | tf_op jit(solution)/shard_map/hqk,khe->qhe/dot_general | solution.py:37
  139.0 13.8 %all-gather.5.cloned.1.call-done = bf16[1408,1408]{1,0:T(8,128)(2,1)} async-done(((bf16[88,1408]{1,0:T(8,128)(2,1)}), bf16[1408,1408]{1,0:T(8,128)(2,1)}) %all-gather.5.cloned.1.call-update) | async-done | bytes 3964944 | tf_op jit(solution)/shard_map/all_gather | solution.py:274
  152.9 5.1 %fusion.26 = (f32[512]{0:T(512)S(1)}, f32[512,1408]{1,0:T(8,128)S(1)}) fusion(f32[1408]{0:T(1024)S(1)} %copy-done.2, bf16[512,1408]{0,1:T(8,128)(2,1)S(1)} %bitcast.28, bf16[1408,1408]{1,0:T(8,128)(2,1)} %all-gather.5.cloned.1.call-done, bf16[512,1408]{1,0:T(8,128)(2,1)S(1)} %copy-done), kind=kOutput, calls=%fused_computation.48 | convolution fusion | flops 2032926208 | bytes 9739776 | tf_op jit(solution)/shard_map/dot_general | solution.py:273
  158.0 0.4 multiply_reduce_fusion
  158.4 0.2 copy-done.3
  158.7 0.5 add_convert_fusion.1
  159.2 0.4 reshape.112
  159.6 1.3 copy.32
  160.9 74.9 %project.1 = (bf16[16,128,256]{2,1,0:T(8,128)(2,1)}, f32[8,128]{1,0:T(8,128)}) custom-call(bf16[4,128,1408]{2,1,0:T(8,128)(2,1)} %bitcast.27, bf16[4,1408,256]{2,1,0:T(8,128)(2,1)} %bitcast.29, f32[1,256]{1,0:T(1,128)} %bitcast.34, s32[16,128]{1,0:T(8,128)} %bitcast.33), custom_call_target="tpu_custom_call" | custom-call | tf_op jit(solution)/shard_map/project/pallas_call | solution.py:235
  235.7 1.3 slice_bitcast_fusion
  237.0 0.2 select_reduce_fusion
  237.2 2.5 %fusion.13 = bf16[2048,256]{1,0:T(8,128)(2,1)} fusion(bf16[16,128,256]{2,1,0:T(8,128)(2,1)} %get-tuple-element.4, f32[2048]{0:T(1024)S(1)} %get-tuple-element.6, pred[2048]{0:T(1024)(128)(4,1)S(1)} %get-tuple-element.7), kind=kLoop, calls=%fused_computation.24 | loop fusion | flops 2097152 | bytes 2107392 | tf_op jit(solution)/shard_map/convert_element_type | solution.py:286
  (27 shorter events, 0.2 us)
Async XLA Ops:
  7.2 3.2 %copy-start = (bf16[512,1408]{1,0:T(8,128)(2,1)S(1)}, bf16[512,1408]{1,0:T(8,128)(2,1)}, u32[]{:S(2)}) copy-start(bf16[512,1408]{1,0:T(8,128)(2,1)} %param.14) | copy-start | bytes 4325380
  7.2 3.7 %copy-start.6 = (s32[512]{0:T(512)S(1)}, s32[512]{0:T(512)}, u32[]{:S(2)}) copy-start(s32[512]{0:T(512)} %param.16) | copy-start | bytes 6148
  7.2 3.7 %copy-start.5 = (s32[512]{0:T(512)S(1)}, s32[512]{0:T(512)}, u32[]{:S(2)}) copy-start(s32[512]{0:T(512)} %param.15) | copy-start | bytes 6148
  7.2 93.3 %copy-start.7 = (f32[4224]{0:T(1024)S(1)}, f32[4224]{0:T(1024)}, u32[]{:S(2)}) copy-start(f32[4224]{0:T(1024)} %param.21) | copy-start | bytes 50692
  7.2 93.3 %copy-start.8 = (f32[1408]{0:T(1024)S(1)}, f32[1408]{0:T(1024)}, u32[]{:S(2)}) copy-start(f32[1408]{0:T(1024)} %param.19) | copy-start | bytes 16900
  7.2 93.3 %copy-start.9 = (f32[1408]{0:T(1024)S(1)}, f32[1408]{0:T(1024)}, u32[]{:S(2)}) copy-start(f32[1408]{0:T(1024)} %param.18) | copy-start | bytes 16900
  7.2 93.2 %all-gather.3.cloned.1.call-start = ((), (), s32[]{:S(2)}) async-start(), calls=%async_computation | async-start | bytes 12638208 | tf_op jit(solution)/shard_map/all_gather | solution.py:270
  8.0 144.9 %all-gather.5.cloned.1.call-start = ((), (), s32[]{:S(2)}) async-start(), calls=%async_computation.1 | async-start | bytes 4212736 | tf_op jit(solution)/shard_map/all_gather | solution.py:274
  131.0 21.9 %copy-start.2 = (f32[1408]{0:T(1024)S(1)}, f32[1408]{0:T(1024)}, u32[]{:S(2)}) copy-start(f32[1408]{0:T(1024)} %param.23) | copy-start | bytes 16900
  158.0 0.7 copy-start.3
  158.0 0.7 copy-start.4
  160.9 76.1 %copy-start.1 = (s32[2048]{0:T(1024)S(1)}, s32[2048]{0:T(1024)}, u32[]{:S(2)}) copy-start(s32[2048]{0:T(1024)} %param.17) | copy-start | bytes 24580
Sparse Core Ops, SparseCore 0:
  10.2 90.2 all-gather.2
  102.6 50.2 all-gather.4
